TPU v7x, 32 devices: a whole 2x2x4 slice. The times are simulated.
32 devices in a mesh: groups: 1, tok: 8 (over z, y), exp: 2 (over x), sub: 2 (over core).
Axes of the slice: x: 2, y: 2, z: 4, core: 2. Of those that a mesh axis runs over, the one named last changes fastest.
Arguments:
- query: bfloat16 [2, 2, 4, 4096], P(('groups', 'sub'), 'exp'), may hold values from -9 to 9, as said below
- key_cache_table: bfloat16 [2, 2, 4, 1024, 512], P(('groups', 'sub'), 'exp', None, 'tok'), may hold values from -9 to 9, as said below
- value_cache_table: bfloat16 [2, 2, 4, 1024, 512], P(('groups', 'sub'), 'exp', None, 'tok'), may hold values from -6 to 6
- latest_key: bfloat16 [2, 2, 4, 512], P(('groups', 'sub'), 'exp'), may hold values from -6 to 6
- latest_value: bfloat16 [2, 2, 4, 512], P(('groups', 'sub'), 'exp'), may hold values from -6 to 6
- lengths: int32 [2, 2, 4], P(('groups', 'sub'), 'exp'), may hold values from 2 to 1024, as said below
- resid: bfloat16 [2, 2, 4, 2048], P(('groups', 'sub'), 'exp', None, 'tok'), may hold values from -250 to 250
- norm_gain: float32 [2048], replicated, may hold values from 0.5 to 1.5
- out_weight: bfloat16 [4096, 2048], P('tok'), may hold values from -0.09375 to 0.09375
- expert_ids: int32 [2, 2, 4, 8], P('groups'), may hold values from 0 to 15, all different within a row; in each aligned block of 16 rows (0 to 15, 16 to 31, ..., all dimensions but the last counted through in order) at most 16 rows name the same one
- gate_weights: float32 [2, 2, 4, 8], P('groups'), may hold values from 0.05 to 0.35
- w_gate: bfloat16 [16, 2048, 768], P(('tok', 'sub'), None, 'exp'), may hold values from -0.125 to 0.125
- w_up: bfloat16 [16, 2048, 768], P(('tok', 'sub'), None, 'exp'), may hold values from -0.125 to 0.125
- w_down: bfloat16 [16, 768, 2048], P(('tok', 'sub'), 'exp'), may hold values from -0.21875 to 0.21875
Outputs:
- attention_out: float32 [2, 2, 4, 2048], P(('groups', 'sub'), 'exp', None, 'tok')
- expert_out: float32 [2, 2, 4, 2048], P('groups', None, None, ('tok', 'exp', 'sub'))
Inputs may be any that keep to these rules, and one draw needn't show every extreme that they name: `query`: most entries are of order one; some rows may align queries of the first key head's query heads with the keys at positions 0 and 1. `key_cache_table`: most entries are of order one. `lengths`: some row reaches 1024. `expert_ids`: each row names 8 different experts; over all 16 rows no expert is named by more than 16 rows, a bound that some block reaches.
All inputs are finite; a program needn't handle non-finite values.
Results may differ from a plain program's by a relative error of at most 0.013.
Values may be sent and summed in bfloat16 or wider, within the bound.
No kernel may reach another device: no remote copies, remote signals or barrier semaphores. Data moves between devices by JAX's collectives and lax.ppermute only.
A program may use at most 64 MiB of HBM per device.

v0:
```python
import jax
import jax.numpy as jnp
from jax import lax
from jax.sharding import PartitionSpec as P

D = 2048
QUERY_HEADS = 32
KEY_VALUE_HEADS = 4
HEAD_DIMENSION = 128
TOPK = 8


def slot_table(chosen_ids, chosen_gates, experts_all, slots_cap):
    expert_iota = lax.broadcasted_iota(jnp.int32, (1, 1, experts_all), 2)
    hits = chosen_ids[:, :, None] == expert_iota
    row_hits = jnp.sum(hits.astype(jnp.int32), axis=1)
    ranks = jnp.cumsum(row_hits, axis=0) - row_hits
    slot_of = jnp.sum(jnp.where(hits, ranks[:, None, :] + expert_iota * slots_cap, 0), axis=2)
    slot_iota = lax.broadcasted_iota(jnp.int32, (1, 1, experts_all * slots_cap), 2)
    weight_map = jnp.sum(
        jnp.where(slot_of[:, :, None] == slot_iota, chosen_gates[:, :, None], 0.0), axis=1
    )
    return (row_hits, ranks, weight_map)


def body(
    query,
    key_cache_table,
    value_cache_table,
    latest_key,
    latest_value,
    lengths,
    resid,
    norm_gain,
    out_weight,
    expert_ids,
    gate_weights,
    w_gate,
    w_up,
    w_down,
):
    tok_ranks = lax.axis_size("tok")
    tok_place = lax.axis_index("tok")
    exp_ranks = lax.axis_size("exp")
    exp_place = lax.axis_index("exp")
    sub_ranks = lax.axis_size("sub")
    sub_place = lax.axis_index("sub")
    sequence_total = query.shape[2]
    local_extent = key_cache_table.shape[3]
    feature_cols = resid.shape[3]
    query_group_width = QUERY_HEADS // KEY_VALUE_HEADS
    own_heads = QUERY_HEADS // tok_ranks
    score_scale = HEAD_DIMENSION ** (-0.5)
    query_rows = query.reshape(sequence_total, KEY_VALUE_HEADS, query_group_width, HEAD_DIMENSION)
    stored_keys = key_cache_table.reshape(
        sequence_total, local_extent, KEY_VALUE_HEADS, HEAD_DIMENSION
    )
    stored_values = value_cache_table.reshape(
        sequence_total, local_extent, KEY_VALUE_HEADS, HEAD_DIMENSION
    )
    scores = (
        jnp.einsum("rhgd,rphd->rhgp", query_rows, stored_keys, preferred_element_type=jnp.float32)
        * score_scale
    )
    position = tok_place * local_extent + lax.broadcasted_iota(
        jnp.int32, (sequence_total, 1, 1, local_extent), 3
    )
    usable = position < lengths.reshape(sequence_total, 1, 1, 1)
    masked = jnp.where(usable, scores, -1e30)
    block_max = jnp.max(masked, axis=3)
    weights = jnp.where(usable, jnp.exp(masked - block_max[..., None]), 0.0).astype(jnp.bfloat16)
    totals = jnp.sum(weights.astype(jnp.float32), axis=3)
    numerator = jnp.einsum(
        "rhgp,rphd->rhgd", weights, stored_values, preferred_element_type=jnp.float32
    )
    partial_value = (
        (numerator / jnp.maximum(totals, 1.0)[..., None])
        .astype(jnp.bfloat16)
        .reshape(sequence_total, 1, QUERY_HEADS, HEAD_DIMENSION)
    )
    arrived_parts = lax.all_to_all(partial_value, "tok", split_axis=2, concat_axis=1, tiled=True)
    arrived_max, arrived_tot = (
        lax.all_to_all(
            block_max.reshape(sequence_total, 1, QUERY_HEADS),
            "tok",
            split_axis=2,
            concat_axis=1,
            tiled=True,
        ),
        lax.all_to_all(
            totals.reshape(sequence_total, 1, QUERY_HEADS),
            "tok",
            split_axis=2,
            concat_axis=1,
            tiled=True,
        ),
    )
    head_ids = tok_place * own_heads + lax.broadcasted_iota(jnp.int32, (own_heads,), 0)
    key_value_choice = head_ids // query_group_width
    own_query = lax.dynamic_slice_in_dim(
        query.reshape(sequence_total, QUERY_HEADS, HEAD_DIMENSION),
        tok_place * own_heads,
        own_heads,
        1,
    )
    incoming_key = jnp.take(
        latest_key.reshape(sequence_total, KEY_VALUE_HEADS, HEAD_DIMENSION),
        key_value_choice,
        axis=1,
    )
    incoming_value = jnp.take(
        latest_value.reshape(sequence_total, KEY_VALUE_HEADS, HEAD_DIMENSION),
        key_value_choice,
        axis=1,
    )
    own_score = (
        jnp.sum(own_query.astype(jnp.float32) * incoming_key.astype(jnp.float32), axis=2)
        * score_scale
    )
    top_score = jnp.maximum(jnp.max(arrived_max, axis=1), own_score)
    factor = arrived_tot * jnp.exp(arrived_max - top_score[:, None, :])
    self_weight = jnp.exp(own_score - top_score)
    combined = jnp.einsum("rbm,rbmd->rmd", factor, arrived_parts.astype(jnp.float32)) + self_weight[
        ..., None
    ] * incoming_value.astype(jnp.float32)
    heads_out = (
        (combined / (jnp.sum(factor, axis=1) + self_weight)[..., None])
        .reshape(sequence_total, own_heads * HEAD_DIMENSION)
        .astype(jnp.bfloat16)
    )
    attended = lax.psum_scatter(
        lax.dot_general(
            out_weight, heads_out, (((0,), (1,)), ((), ())), preferred_element_type=jnp.float32
        ),
        "tok",
        scatter_dimension=0,
        tiled=True,
    ).T
    hidden_part = resid.reshape(sequence_total, feature_cols).astype(jnp.float32) + attended
    hidden_full = lax.all_gather(hidden_part, "tok", axis=1, tiled=True)
    normed = (
        hidden_full
        * lax.rsqrt(jnp.mean(hidden_full * hidden_full, axis=1, keepdims=True) + 1e-06)
        * norm_gain
    ).astype(jnp.bfloat16)
    source_rows = lax.all_gather(
        normed.reshape(1, sequence_total, D), ("exp", "sub"), axis=0, tiled=True
    ).reshape(-1, D)
    rows_total = exp_ranks * sub_ranks * sequence_total
    experts_all = tok_ranks * sub_ranks
    slots_cap = min(rows_total, max(2, 2 * rows_total * TOPK // experts_all))
    block_cols = D // (tok_ranks * exp_ranks * sub_ranks)
    chosen_ids = jnp.transpose(expert_ids, (1, 0, 2, 3)).reshape(rows_total, TOPK)
    chosen_gates = jnp.transpose(gate_weights, (1, 0, 2, 3)).reshape(rows_total, TOPK)
    row_hits, ranks, weight_map = slot_table(chosen_ids, chosen_gates, experts_all, slots_cap)
    my_expert = tok_place * sub_ranks + sub_place
    my_hits = lax.dynamic_slice_in_dim(row_hits, my_expert, 1, 1)
    my_ranks = lax.dynamic_slice_in_dim(ranks, my_expert, 1, 1)
    slot_iota = lax.broadcasted_iota(jnp.int32, (1, slots_cap), 1)
    picker = ((my_ranks == slot_iota) & (my_hits > 0)).astype(jnp.bfloat16)
    picked = lax.dot_general(
        picker, source_rows, (((0,), (0,)), ((), ())), preferred_element_type=jnp.float32
    ).astype(jnp.bfloat16)
    gate_proj = jnp.dot(picked, w_gate[0], preferred_element_type=jnp.float32)
    up_proj = jnp.dot(picked, w_up[0], preferred_element_type=jnp.float32)
    active = (jax.nn.silu(gate_proj) * up_proj).astype(jnp.bfloat16)
    slice_out = jnp.dot(active, w_down[0], preferred_element_type=jnp.float32)
    summed = lax.psum(slice_out, "exp").astype(jnp.bfloat16)
    mine = lax.dynamic_slice_in_dim(
        summed.reshape(slots_cap, tok_ranks, exp_ranks, sub_ranks, block_cols), exp_place, 1, 2
    )
    expert_y = mine.reshape(slots_cap, tok_ranks * sub_ranks, block_cols)
    received = lax.all_to_all(expert_y, ("tok", "sub"), split_axis=1, concat_axis=0, tiled=True)
    received = (
        lax.optimization_barrier(received)
        .astype(jnp.float32)
        .reshape(experts_all * slots_cap, block_cols)
    )
    mixed = jnp.dot(weight_map, received, precision=lax.Precision.HIGHEST)
    expert_mix = jnp.transpose(
        mixed.reshape(exp_ranks, sub_ranks, sequence_total, block_cols), (1, 0, 2, 3)
    )
    return (attended.reshape(1, 1, sequence_total, feature_cols), expert_mix)


def solution(mesh):
    placed = (
        P(("groups", "sub"), "exp", None, None),
        P(("groups", "sub"), "exp", None, "tok", None),
        P(("groups", "sub"), "exp", None, "tok", None),
        P(("groups", "sub"), "exp", None, None),
        P(("groups", "sub"), "exp", None, None),
        P(("groups", "sub"), "exp", None),
        P(("groups", "sub"), "exp", None, "tok"),
        P(),
        P("tok", None),
        P("groups", None, None, None),
        P("groups", None, None, None),
        P(("tok", "sub"), None, "exp"),
        P(("tok", "sub"), None, "exp"),
        P(("tok", "sub"), "exp", None),
    )
    return jax.shard_map(
        body,
        mesh=mesh,
        in_specs=placed,
        out_specs=(
            P(("groups", "sub"), "exp", None, "tok"),
            P("groups", None, None, ("tok", "exp", "sub")),
        ),
        check_vma=False,
    )
```

profile of v0, /device:TPU:0, one launch (start us, length us, event | category | flops | bytes accessed | tf_op | source)
XLA Modules:
  0.0 179.8 jit_solution(13984810057513307680)
XLA Ops:
  7.2 0.0 copy-start
  7.2 0.0 copy-start.1
  7.2 0.0 copy-start.4
  7.2 0.0 copy-start.6
  7.2 1.3 reshape.165
  8.5 0.0 copy-start.7
  8.6 0.0 copy-start.5
  8.6 0.7 broadcast_compare_fusion
  9.3 1.2 fusion.51
  10.5 0.7 copy.79
  11.2 7.3 %all-to-all-start.1 = ((f32[4,1,32]{0,1,2:T(1,128)}), f32[4,1,32]{0,1,2:T(1,128)S(1)}, u32[]{:S(2)}, u32[]{:S(2)}) async-start(f32[4,1,32]{0,1,2:T(1,128)} %bitcast.3), calls=%async_computation.1 | async-start | bytes 32768 | tf_op jit(solution)/shard_map/all_to_all | solution.py:83
  18.6 0.2 convert_reduce_fusion.1
  18.8 0.0 copy-done.1
  18.8 0.1 reshape.170
  18.9 0.0 copy-done.4
  19.0 0.1 convert_reduce_fusion
  19.1 0.0 copy-done.6
  19.1 0.6 gather_fusion
  19.7 0.3 fusion.8
  20.0 0.9 multiply_reduce_fusion.1
  20.8 0.7 copy.77
  21.5 0.1 copy.63
  21.6 0.6 copy.65
  22.2 0.0 copy-done.7
  22.3 0.6 gather_fusion.1
  22.8 2.3 %all-to-all-done.1 = f32[4,1,32]{0,1,2:T(1,128)S(1)} async-done(((f32[4,1,32]{0,1,2:T(1,128)}), f32[4,1,32]{0,1,2:T(1,128)S(1)}, u32[]{:S(2)}, u32[]{:S(2)}) %all-to-all-start.1) | async-done | bytes 544 | tf_op jit(solution)/shard_map/all_to_all | solution.py:83
  25.1 3.7 %all-to-all-start = ((f32[4,1,32]{0,1,2:T(1,128)}), f32[4,1,32]{0,1,2:T(1,128)S(1)}, u32[]{:S(2)}, u32[]{:S(2)}) async-start(f32[4,1,32]{0,1,2:T(1,128)} %bitcast.1), calls=%async_computation | async-start | bytes 32768 | tf_op jit(solution)/shard_map/all_to_all | solution.py:90
  28.9 0.2 dynamic-slice_reduce_fusion
  29.0 0.2 fusion.35
  29.2 0.1 copy.80
  29.4 0.1 copy.84
  29.5 5.9 %all-to-all-done = f32[4,1,32]{0,1,2:T(1,128)S(1)} async-done(((f32[4,1,32]{0,1,2:T(1,128)}), f32[4,1,32]{0,1,2:T(1,128)S(1)}, u32[]{:S(2)}, u32[]{:S(2)}) %all-to-all-start) | async-done | bytes 544 | tf_op jit(solution)/shard_map/all_to_all | solution.py:90
  35.4 3.3 %all-to-all-start.2 = ((bf16[4,1,32,128]{3,0,1,2:T(4,128)(2,1)}), bf16[4,1,32,128]{3,0,1,2:T(4,128)(2,1)S(1)}, u32[]{:S(2)}, u32[]{:S(2)}) async-start(bf16[4,1,32,128]{3,0,1,2:T(4,128)(2,1)} %copy.65), calls=%async_computation.2 | async-start | bytes 65536 | tf_op jit(solution)/shard_map/all_to_all | solution.py:81
  38.8 0.0 reduce-scatter.4.cloned.1.call-start
  38.8 0.1 copy.78
  39.0 0.1 copy.66
  39.1 0.1 copy.67
  39.2 0.1 copy.73
  39.3 6.1 %all-to-all-done.2 = bf16[4,1,32,128]{3,0,1,2:T(4,128)(2,1)S(1)} async-done(((bf16[4,1,32,128]{3,0,1,2:T(4,128)(2,1)}), bf16[4,1,32,128]{3,0,1,2:T(4,128)(2,1)S(1)}, u32[]{:S(2)}, u32[]{:S(2)}) %all-to-all-start.2) | async-done | bytes 32800 | tf_op jit(solution)/shard_map/all_to_all | solution.py:81
  45.4 0.1 fusion.22
  45.5 0.4 convolution_bitcast_fusion
  46.0 1.4 copy.82
  47.3 0.0 reduce-scatter.4.cloned.1.call-update
  47.4 0.4 select_reduce_fusion.1
  47.8 61.6 %reduce-scatter.4.cloned.1.call-done = f32[256,4]{1,0:T(8,128)} async-done(((f32[2048,4]{1,0:T(8,128)}), f32[256,4]{1,0:T(8,128)}) %reduce-scatter.4.cloned.1.call-update) | async-done | bytes 4112
  109.4 1.0 copy.83
  110.4 30.6 %all_gather.6 = f32[4,2048]{1,0:T(4,128)S(1)} all-gather(f32[4,256]{1,0:T(4,128)S(1)} %convert_add_fusion), channel_id=1, replica_groups=mesh['groups'=1,'tok'=8,'exp'=2,'sub'=2] {'tok'}, dimensions={1}, use_global_device_ids=true | all-gather | bytes 36864 | tf_op jit(solution)/shard_map/all_gather | solution.py:140
  141.0 0.1 multiply_reduce_fusion
  141.2 0.1 fusion.29
  141.2 5.2 %all-gather.1 = bf16[4,4,2048]{2,1,0:T(4,128)(2,1)S(1)} all-gather(bf16[1,4,2048]{2,1,0:T(4,128)(2,1)S(1)} %fusion.29), channel_id=2, replica_groups=mesh['groups'=1,'tok'=8,'exp'=2,'sub'=2] {'exp','sub'}, dimensions={0}, use_global_device_ids=true | all-gather | bytes 81920 | tf_op jit(solution)/shard_map/all_gather | solution.py:146
  146.5 0.3 convolution_convert_fusion
  146.8 1.7 fusion.4
  148.5 2.6 %fusion = f32[16,2048]{1,0:T(8,128)S(1)} fusion(bf16[1,384,2048]{2,1,0:T(8,128)(2,1)} %param.29, bf16[16,2048]{1,0:T(8,128)(2,1)S(1)} %convolution_convert_fusion, bf16[1,2048,384]{2,1,0:T(8,128)(2,1)} %param.28, f32[16,384]{1,0:T(8,128)S(1)} %fusion.4), kind=kOutput, calls=%fused_computation.4 | convolution fusion | flops 50368512 | bytes 3366912 | tf_op jit(solution)/shard_map/dot_general | solution.py:167
  151.1 0.0 copy-done.2
  151.1 9.7 %all-reduce.1 = bf16[16,2048]{1,0:T(8,128)(2,1)S(1)} all-reduce(f32[16,2048]{1,0:T(8,128)S(1)} %fusion), channel_id=1, replica_groups=mesh['groups'=1,'tok'=8,'exp'=2,'sub'=2] {'exp'}, use_global_device_ids=true, to_apply=%region_11.13 | all-reduce | flops 32768 | bytes 196608 | tf_op jit(solution)/shard_map/psum | solution.py:168
  160.9 0.2 reshape.176
  161.1 0.1 constant_dynamic-slice_fusion
  161.2 0.7 reshape.213
  161.9 3.5 %all-to-all-start.3 = ((bf16[16,2,512]{2,1,0:T(2,128)(2,1)}), bf16[16,2,512]{2,1,0:T(2,128)(2,1)S(1)}, u32[]{:S(2)}, u32[]{:S(2)}) async-start(bf16[16,2,512]{2,1,0:T(2,128)(2,1)} %reshape.213), calls=%async_computation.3 | async-start | bytes 65536 | tf_op jit(solution)/shard_map/all_to_all | solution.py:173
  165.4 0.1 select_reduce_fusion
  165.6 6.5 %all-to-all-done.3 = bf16[16,2,512]{2,1,0:T(2,128)(2,1)S(1)} async-done(((bf16[16,2,512]{2,1,0:T(2,128)(2,1)}), bf16[16,2,512]{2,1,0:T(2,128)(2,1)S(1)}, u32[]{:S(2)}, u32[]{:S(2)}) %all-to-all-start.3) | async-done | bytes 32800 | tf_op jit(solution)/shard_map/all_to_all | solution.py:173
  172.1 0.1 reshape.214
  172.2 0.1 convolution_bitcast_fusion.1
  172.3 0.6 copy.72
  (27 shorter events, 0.2 us)
Async XLA Ops:
  7.2 38.4 %copy-start = (bf16[512,2048]{1,0:T(8,128)(2,1)S(1)}, bf16[512,2048]{1,0:T(8,128)(2,1)}, u32[]{:S(2)}) copy-start(bf16[512,2048]{1,0:T(8,128)(2,1)} %param.24) | copy-start | bytes 6291460
  7.2 11.6 %copy-start.1 = (bf16[1,1,4,128,512]{4,3,2,1,0:T(8,128)(2,1)S(1)}, bf16[1,1,4,128,512]{4,3,2,1,0:T(8,128)(2,1)}, u32[]{:S(2)}) copy-start(bf16[1,1,4,128,512]{4,3,2,1,0:T(8,128)(2,1)} %param.18) | copy-start | bytes 1572868
  7.2 11.8 %copy-start.4 = (s32[2,2,4,8]{3,2,1,0:T(4,128)S(1)}, s32[2,2,4,8]{3,2,1,0:T(4,128)}, u32[]{:S(2)}) copy-start(s32[2,2,4,8]{3,2,1,0:T(4,128)} %param.25) | copy-start | bytes 1540
  7.2 11.9 %copy-start.6 = (bf16[1,1,4,512]{3,2,1,0:T(4,128)(2,1)S(1)}, bf16[1,1,4,512]{3,2,1,0:T(4,128)(2,1)}, u32[]{:S(2)}) copy-start(bf16[1,1,4,512]{3,2,1,0:T(4,128)(2,1)} %param.19) | copy-start | bytes 12292
  8.5 13.7 %copy-start.7 = (bf16[1,1,4,512]{3,2,1,0:T(4,128)(2,1)S(1)}, bf16[1,1,4,512]{3,2,1,0:T(4,128)(2,1)}, u32[]{:S(2)}) copy-start(bf16[1,1,4,512]{3,2,1,0:T(4,128)(2,1)} %param.20) | copy-start | bytes 12292
  8.6 20.3 %copy-start.5 = (f32[2,2,4,8]{3,2,1,0:T(4,128)S(1)}, f32[2,2,4,8]{3,2,1,0:T(4,128)}, u32[]{:S(2)}) copy-start(f32[2,2,4,8]{3,2,1,0:T(4,128)} %param.26) | copy-start | bytes 1540
  11.2 13.9 %all-to-all-start.1 = ((f32[4,1,32]{0,1,2:T(1,128)}), f32[4,1,32]{0,1,2:T(1,128)S(1)}, u32[]{:S(2)}, u32[]{:S(2)}) async-start(f32[4,1,32]{0,1,2:T(1,128)} %bitcast.3), calls=%async_computation.1 | async-start | bytes 32768 | tf_op jit(solution)/shard_map/all_to_all | solution.py:83
  25.1 10.3 %all-to-all-start = ((f32[4,1,32]{0,1,2:T(1,128)}), f32[4,1,32]{0,1,2:T(1,128)S(1)}, u32[]{:S(2)}, u32[]{:S(2)}) async-start(f32[4,1,32]{0,1,2:T(1,128)} %bitcast.1), calls=%async_computation | async-start | bytes 32768 | tf_op jit(solution)/shard_map/all_to_all | solution.py:90
  35.4 10.0 %all-to-all-start.2 = ((bf16[4,1,32,128]{3,0,1,2:T(4,128)(2,1)}), bf16[4,1,32,128]{3,0,1,2:T(4,128)(2,1)S(1)}, u32[]{:S(2)}, u32[]{:S(2)}) async-start(bf16[4,1,32,128]{3,0,1,2:T(4,128)(2,1)} %copy.65), calls=%async_computation.2 | async-start | bytes 65536 | tf_op jit(solution)/shard_map/all_to_all | solution.py:81
  38.8 70.7 %reduce-scatter.4.cloned.1.call-start = ((), (), s32[]{:S(2)}) async-start(), calls=%async_computation.5 | async-start | bytes 1179648
  46.0 64.4 %copy-start.8 = (bf16[1,1,4,256]{3,2,1,0:T(4,128)(2,1)S(1)}, bf16[1,1,4,256]{3,2,1,0:T(4,128)(2,1)}, u32[]{:S(2)}) copy-start(bf16[1,1,4,256]{3,2,1,0:T(4,128)(2,1)} %param.22) | copy-start | bytes 6148
  46.0 95.2 %copy-start.3 = (f32[2048]{0:T(1024)S(1)}, f32[2048]{0:T(1024)}, u32[]{:S(2)}) copy-start(f32[2048]{0:T(1024)} %param.23) | copy-start | bytes 24580
  110.4 40.7 %copy-start.2 = (f32[256,4]{0,1:T(4,128)}, f32[256,4]{0,1:T(4,128)S(1)}, u32[]{:S(2)}) copy-start(f32[256,4]{0,1:T(4,128)S(1)} %copy.83) | copy-start | bytes 12292
  161.9 10.2 %all-to-all-start.3 = ((bf16[16,2,512]{2,1,0:T(2,128)(2,1)}), bf16[16,2,512]{2,1,0:T(2,128)(2,1)S(1)}, u32[]{:S(2)}, u32[]{:S(2)}) async-start(bf16[16,2,512]{2,1,0:T(2,128)(2,1)} %reshape.213), calls=%async_computation.3 | async-start | bytes 65536 | tf_op jit(solution)/shard_map/all_to_all | solution.py:173
Sparse Core Ops, SparseCore 0:
  47.5 61.8 reduce-scatter.3
where the time goes:
time: 180 us
  waiting for transfers between devices  82.4 us (46%)
  blocking collectives  45.6 us (25%)
  starting transfers between devices  17.9 us (10%)
  between operations  14.3 us (8%)
  local copies, waits for them, and re-layouts  9.66 us (5%)
  matrix products  6.85 us (4%)
  other arithmetic  2.97 us (2%)
    unnamed x2, waiting for transfers between devices  61.7 us
    all_gather x1, blocking collectives, body(): hidden_full = lax.all_gather(hidden_part, 'tok', axis=1, tiled=True)  30.6 us
    psum x1, blocking collectives, body(): summed = lax.psum(slice_out, 'exp').astype(jnp.bfloat16)  9.75 us
    all_to_all x1, starting transfers between devices, body(): lax.all_to_all(block_max.reshape(sequence_total, 1, QUERY_HEADS), 'tok',...  7.31 us
    all_to_all x1, waiting for transfers between devices, body(): lax.all_to_all(expert_y, ('tok', 'sub'), split_axis=1, concat_axis=0, til...  6.49 us
    all_to_all x1, waiting for transfers between devices, body(): lax.all_to_all(partial_value, 'tok', split_axis=2, concat_axis=1, tiled=T...  6.05 us
    all_to_all x1, waiting for transfers between devices, body(): lax.all_to_all(totals.reshape(sequence_total, 1, QUERY_HEADS), 'tok', spl...  5.94 us
    all_gather x1, blocking collectives, body(): lax.all_gather(normed.reshape(1, sequence_total, D), ('exp', 'sub'), axis...  5.23 us
  transfers between devices with their start and end apart: 5, of which 5 were waited for; matrix products, arithmetic and copies ran while one was open for 3% of the time, Pallas kernels for 0%

commit v1 on v0

--- a/solution.py
+++ b/solution.py
@@ -87,12 +87,18 @@
             concat_axis=1,
             tiled=True,
         ),
-        lax.all_to_all(
-            totals.reshape(sequence_total, 1, QUERY_HEADS),
-            "tok",
-            split_axis=2,
-            concat_axis=1,
-            tiled=True,
+        jnp.concatenate(
+            lax.all_to_all(
+                jnp.stack(
+                    jnp.split(
+                        totals.reshape(sequence_total, 1, QUERY_HEADS), lax.axis_size("tok"), axis=2
+                    )
+                ),
+                "tok",
+                0,
+                0,
+            ),
+            axis=1,
         ),
     )
     head_ids = tok_place * own_heads + lax.broadcasted_iota(jnp.int32, (own_heads,), 0)

time: 180 us -> 185 us (1.028)
  local copies, waits for them, and re-layouts: 9.66 us -> 14 us
    unnamed x26 -> x33, local copies, waits for them, and re-layouts: 3.94 us -> 8.45 us
    all_to_all x1, starting transfers between devices: 7.31 us -> 3.53 us  [body(): lax.all_to_all(block_max.reshape(sequence_total, 1, QUERY_HEADS), 'tok',...]
    all_to_all x1, waiting for transfers between devices: 2.3 us -> 6.08 us  [body(): lax.all_to_all(block_max.reshape(sequence_total, 1, QUERY_HEADS), 'tok',...]
    all_to_all x1, starting transfers between devices: 3.72 us -> 7.31 us  [body(): lax.all_to_all(jnp.stack(jnp.split(totals.reshape(sequence_total, 1, QUER...]
    all_to_all x1, waiting for transfers between devices: 5.94 us -> 2.49 us  [body(): lax.all_to_all(jnp.stack(jnp.split(totals.reshape(sequence_total, 1, QUER...]
where the time goes in v1:
time: 185 us; the launch traced here: 184 us
  waiting for transfers between devices  82.7 us (45%)
  blocking collectives  45.6 us (25%)
  starting transfers between devices  17.8 us (10%)
  between operations  14.3 us (8%)
  local copies, waits for them, and re-layouts  14 us (8%)
  matrix products  6.86 us (4%)
  other arithmetic  3.12 us (2%)
    unnamed x2, waiting for transfers between devices  61.7 us
    all_gather x1, blocking collectives, body(): hidden_full = lax.all_gather(hidden_part, 'tok', axis=1, tiled=True)  30.6 us
    psum x1, blocking collectives, body(): summed = lax.psum(slice_out, 'exp').astype(jnp.bfloat16)  9.75 us
    unnamed x33, local copies, waits for them, and re-layouts  8.45 us
    all_to_all x1, starting transfers between devices, body(): lax.all_to_all(jnp.stack(jnp.split(totals.reshape(sequence_total, 1, QUER...  7.31 us
    all_to_all x1, waiting for transfers between devices, body(): lax.all_to_all(expert_y, ('tok', 'sub'), split_axis=1, concat_axis=0, til...  6.49 us
    all_to_all x1, waiting for transfers between devices, body(): lax.all_to_all(block_max.reshape(sequence_total, 1, QUERY_HEADS), 'tok',...  6.08 us
    all_to_all x1, waiting for transfers between devices, body(): lax.all_to_all(partial_value, 'tok', split_axis=2, concat_axis=1, tiled=T...  5.98 us
  transfers between devices with their start and end apart: 5, of which 5 were waited for; matrix products, arithmetic and copies ran while one was open for 3% of the time, Pallas kernels for 0%

profile of v1, /device:TPU:0, one launch (start us, length us, event | category | flops | bytes accessed | tf_op | source)
XLA Modules:
  0.0 184.4 jit_solution(6295038804937707798)
XLA Ops:
  7.2 0.0 copy-start
  7.2 1.3 reshape.165
  8.6 0.0 copy-start.7
  8.6 0.0 copy-start.5
  8.6 0.7 broadcast_compare_fusion
  9.3 1.2 fusion.50
  10.5 0.2 convert_reduce_fusion.1
  10.7 0.1 reshape.166
  10.8 0.6 constant_dynamic-update-slice_fusion.7
  11.4 0.7 constant_dynamic-update-slice_fusion.6
  12.1 0.6 constant_dynamic-update-slice_fusion.5
  12.7 0.7 constant_dynamic-update-slice_fusion.4
  13.4 0.7 constant_dynamic-update-slice_fusion.3
  14.0 0.6 constant_dynamic-update-slice_fusion.2
  14.7 0.7 constant_dynamic-update-slice_fusion.1
  15.3 0.6 constant_dynamic-update-slice_fusion
  16.0 7.3 %all-to-all-start = ((f32[8,4,1,4]{3,1,2,0:T(4,128)}), f32[8,4,1,4]{3,1,2,0:T(4,128)S(1)}, u32[]{:S(2)}, u32[]{:S(2)}) async-start(f32[8,4,1,4]{3,1,2,0:T(4,128)} %constant_dynamic-update-slice_fusion), calls=%async_computation | async-start | bytes 32768 | tf_op jit(solution)/shard_map/all_to_all | solution.py:91
  23.3 0.1 reshape.172
  23.5 0.1 convert_reduce_fusion
  23.6 0.6 gather_fusion
  24.2 0.3 fusion.8
  24.5 0.9 multiply_reduce_fusion.1
  25.4 0.7 copy.81
  26.1 0.1 copy.66
  26.2 0.6 copy.69
  26.8 0.6 gather_fusion.1
  27.4 2.5 %all-to-all-done = f32[8,4,1,4]{3,1,2,0:T(4,128)S(1)} async-done(((f32[8,4,1,4]{3,1,2,0:T(4,128)}), f32[8,4,1,4]{3,1,2,0:T(4,128)S(1)}, u32[]{:S(2)}, u32[]{:S(2)}) %all-to-all-start) | async-done | bytes 544 | tf_op jit(solution)/shard_map/all_to_all | solution.py:91
  29.8 3.5 %all-to-all-start.1 = ((f32[4,1,32]{0,1,2:T(1,128)}), f32[4,1,32]{0,1,2:T(1,128)S(1)}, u32[]{:S(2)}, u32[]{:S(2)}) async-start(f32[4,1,32]{0,1,2:T(1,128)} %bitcast.11), calls=%async_computation.1 | async-start | bytes 32768 | tf_op jit(solution)/shard_map/all_to_all | solution.py:83
  33.4 0.2 dynamic-slice_reduce_fusion
  33.6 0.2 fusion.35
  33.8 0.1 copy.63
  33.9 6.1 %all-to-all-done.1 = f32[4,1,32]{0,1,2:T(1,128)S(1)} async-done(((f32[4,1,32]{0,1,2:T(1,128)}), f32[4,1,32]{0,1,2:T(1,128)S(1)}, u32[]{:S(2)}, u32[]{:S(2)}) %all-to-all-start.1) | async-done | bytes 544 | tf_op jit(solution)/shard_map/all_to_all | solution.py:83
  39.9 3.3 %all-to-all-start.2 = ((bf16[4,1,32,128]{3,0,1,2:T(4,128)(2,1)}), bf16[4,1,32,128]{3,0,1,2:T(4,128)(2,1)S(1)}, u32[]{:S(2)}, u32[]{:S(2)}) async-start(bf16[4,1,32,128]{3,0,1,2:T(4,128)(2,1)} %copy.69), calls=%async_computation.2 | async-start | bytes 65536 | tf_op jit(solution)/shard_map/all_to_all | solution.py:81
  43.3 0.0 reduce-scatter.4.cloned.1.call-start
  43.3 0.1 copy.67
  43.5 0.1 copy.87
  43.6 0.2 fusion.49
  43.7 0.1 copy.70
  43.8 0.1 copy.71
  43.9 6.0 %all-to-all-done.2 = bf16[4,1,32,128]{3,0,1,2:T(4,128)(2,1)S(1)} async-done(((bf16[4,1,32,128]{3,0,1,2:T(4,128)(2,1)}), bf16[4,1,32,128]{3,0,1,2:T(4,128)(2,1)S(1)}, u32[]{:S(2)}, u32[]{:S(2)}) %all-to-all-start.2) | async-done | bytes 32800 | tf_op jit(solution)/shard_map/all_to_all | solution.py:81
  49.9 0.1 fusion.22
  50.0 0.4 convolution_bitcast_fusion
  50.5 1.4 copy.85
  51.9 0.0 reduce-scatter.4.cloned.1.call-update
  51.9 0.4 select_reduce_fusion.1
  52.3 61.7 %reduce-scatter.4.cloned.1.call-done = f32[256,4]{1,0:T(8,128)} async-done(((f32[2048,4]{1,0:T(8,128)}), f32[256,4]{1,0:T(8,128)}) %reduce-scatter.4.cloned.1.call-update) | async-done | bytes 4112
  114.0 1.0 copy.86
  115.0 30.6 %all_gather.6 = f32[4,2048]{1,0:T(4,128)S(1)} all-gather(f32[4,256]{1,0:T(4,128)S(1)} %convert_add_fusion), channel_id=1, replica_groups=mesh['groups'=1,'tok'=8,'exp'=2,'sub'=2] {'tok'}, dimensions={1}, use_global_device_ids=true | all-gather | bytes 36864 | tf_op jit(solution)/shard_map/all_gather | solution.py:146
  145.6 0.1 multiply_reduce_fusion
  145.7 0.1 fusion.29
  145.8 5.2 %all-gather.1 = bf16[4,4,2048]{2,1,0:T(4,128)(2,1)S(1)} all-gather(bf16[1,4,2048]{2,1,0:T(4,128)(2,1)S(1)} %fusion.29), channel_id=2, replica_groups=mesh['groups'=1,'tok'=8,'exp'=2,'sub'=2] {'exp','sub'}, dimensions={0}, use_global_device_ids=true | all-gather | bytes 81920 | tf_op jit(solution)/shard_map/all_gather | solution.py:152
  151.1 0.3 convolution_convert_fusion
  151.3 1.7 fusion.4
  153.1 2.6 %fusion = f32[16,2048]{1,0:T(8,128)S(1)} fusion(bf16[1,384,2048]{2,1,0:T(8,128)(2,1)} %param.29, bf16[16,2048]{1,0:T(8,128)(2,1)S(1)} %convolution_convert_fusion, bf16[1,2048,384]{2,1,0:T(8,128)(2,1)} %param.28, f32[16,384]{1,0:T(8,128)S(1)} %fusion.4), kind=kOutput, calls=%fused_computation.4 | convolution fusion | flops 50368512 | bytes 3366912 | tf_op jit(solution)/shard_map/dot_general | solution.py:173
  155.7 9.7 %all-reduce.1 = bf16[16,2048]{1,0:T(8,128)(2,1)S(1)} all-reduce(f32[16,2048]{1,0:T(8,128)S(1)} %fusion), channel_id=1, replica_groups=mesh['groups'=1,'tok'=8,'exp'=2,'sub'=2] {'exp'}, use_global_device_ids=true, to_apply=%region_11.13 | all-reduce | flops 32768 | bytes 196608 | tf_op jit(solution)/shard_map/psum | solution.py:174
  165.4 0.2 reshape.178
  165.6 0.1 constant_dynamic-slice_fusion
  165.7 0.7 reshape.215
  166.4 3.6 %all-to-all-start.3 = ((bf16[16,2,512]{2,1,0:T(2,128)(2,1)}), bf16[16,2,512]{2,1,0:T(2,128)(2,1)S(1)}, u32[]{:S(2)}, u32[]{:S(2)}) async-start(bf16[16,2,512]{2,1,0:T(2,128)(2,1)} %reshape.215), calls=%async_computation.3 | async-start | bytes 65536 | tf_op jit(solution)/shard_map/all_to_all | solution.py:179
  170.0 0.1 select_reduce_fusion
  170.2 6.5 %all-to-all-done.3 = bf16[16,2,512]{2,1,0:T(2,128)(2,1)S(1)} async-done(((bf16[16,2,512]{2,1,0:T(2,128)(2,1)}), bf16[16,2,512]{2,1,0:T(2,128)(2,1)S(1)}, u32[]{:S(2)}, u32[]{:S(2)}) %all-to-all-start.3) | async-done | bytes 32800 | tf_op jit(solution)/shard_map/all_to_all | solution.py:179
  176.7 0.1 reshape.216
  176.8 0.1 convolution_bitcast_fusion.1
  176.9 0.6 copy.76
  (33 shorter events, 0.2 us)
Async XLA Ops:
  7.2 42.9 %copy-start = (bf16[512,2048]{1,0:T(8,128)(2,1)S(1)}, bf16[512,2048]{1,0:T(8,128)(2,1)}, u32[]{:S(2)}) copy-start(bf16[512,2048]{1,0:T(8,128)(2,1)} %param.24) | copy-start | bytes 6291460
  7.2 16.2 %copy-start.1 = (bf16[1,1,4,128,512]{4,3,2,1,0:T(8,128)(2,1)S(1)}, bf16[1,1,4,128,512]{4,3,2,1,0:T(8,128)(2,1)}, u32[]{:S(2)}) copy-start(bf16[1,1,4,128,512]{4,3,2,1,0:T(8,128)(2,1)} %param.18) | copy-start | bytes 1572868
  7.2 16.3 %copy-start.4 = (s32[2,2,4,8]{3,2,1,0:T(4,128)S(1)}, s32[2,2,4,8]{3,2,1,0:T(4,128)}, u32[]{:S(2)}) copy-start(s32[2,2,4,8]{3,2,1,0:T(4,128)} %param.25) | copy-start | bytes 1540
  7.2 16.4 %copy-start.6 = (bf16[1,1,4,512]{3,2,1,0:T(4,128)(2,1)S(1)}, bf16[1,1,4,512]{3,2,1,0:T(4,128)(2,1)}, u32[]{:S(2)}) copy-start(bf16[1,1,4,512]{3,2,1,0:T(4,128)(2,1)} %param.19) | copy-start | bytes 12292
  8.6 18.2 %copy-start.7 = (bf16[1,1,4,512]{3,2,1,0:T(4,128)(2,1)S(1)}, bf16[1,1,4,512]{3,2,1,0:T(4,128)(2,1)}, u32[]{:S(2)}) copy-start(bf16[1,1,4,512]{3,2,1,0:T(4,128)(2,1)} %param.20) | copy-start | bytes 12292
  8.6 24.8 %copy-start.5 = (f32[2,2,4,8]{3,2,1,0:T(4,128)S(1)}, f32[2,2,4,8]{3,2,1,0:T(4,128)}, u32[]{:S(2)}) copy-start(f32[2,2,4,8]{3,2,1,0:T(4,128)} %param.26) | copy-start | bytes 1540
  16.0 13.9 %all-to-all-start = ((f32[8,4,1,4]{3,1,2,0:T(4,128)}), f32[8,4,1,4]{3,1,2,0:T(4,128)S(1)}, u32[]{:S(2)}, u32[]{:S(2)}) async-start(f32[8,4,1,4]{3,1,2,0:T(4,128)} %constant_dynamic-update-slice_fusion), calls=%async_computation | async-start | bytes 32768 | tf_op jit(solution)/shard_map/all_to_all | solution.py:91
  29.8 10.1 %all-to-all-start.1 = ((f32[4,1,32]{0,1,2:T(1,128)}), f32[4,1,32]{0,1,2:T(1,128)S(1)}, u32[]{:S(2)}, u32[]{:S(2)}) async-start(f32[4,1,32]{0,1,2:T(1,128)} %bitcast.11), calls=%async_computation.1 | async-start | bytes 32768 | tf_op jit(solution)/shard_map/all_to_all | solution.py:83
  39.9 10.0 %all-to-all-start.2 = ((bf16[4,1,32,128]{3,0,1,2:T(4,128)(2,1)}), bf16[4,1,32,128]{3,0,1,2:T(4,128)(2,1)S(1)}, u32[]{:S(2)}, u32[]{:S(2)}) async-start(bf16[4,1,32,128]{3,0,1,2:T(4,128)(2,1)} %copy.69), calls=%async_computation.2 | async-start | bytes 65536 | tf_op jit(solution)/shard_map/all_to_all | solution.py:81
  43.3 70.7 %reduce-scatter.4.cloned.1.call-start = ((), (), s32[]{:S(2)}) async-start(), calls=%async_computation.5 | async-start | bytes 1179648
  50.5 64.5 %copy-start.8 = (bf16[1,1,4,256]{3,2,1,0:T(4,128)(2,1)S(1)}, bf16[1,1,4,256]{3,2,1,0:T(4,128)(2,1)}, u32[]{:S(2)}) copy-start(bf16[1,1,4,256]{3,2,1,0:T(4,128)(2,1)} %param.22) | copy-start | bytes 6148
  50.5 95.2 %copy-start.3 = (f32[2048]{0:T(1024)S(1)}, f32[2048]{0:T(1024)}, u32[]{:S(2)}) copy-start(f32[2048]{0:T(1024)} %param.23) | copy-start | bytes 24580
  114.9 40.7 %copy-start.2 = (f32[256,4]{0,1:T(4,128)}, f32[256,4]{0,1:T(4,128)S(1)}, u32[]{:S(2)}) copy-start(f32[256,4]{0,1:T(4,128)S(1)} %copy.86) | copy-start | bytes 12292
  166.4 10.2 %all-to-all-start.3 = ((bf16[16,2,512]{2,1,0:T(2,128)(2,1)}), bf16[16,2,512]{2,1,0:T(2,128)(2,1)S(1)}, u32[]{:S(2)}, u32[]{:S(2)}) async-start(bf16[16,2,512]{2,1,0:T(2,128)(2,1)} %reshape.215), calls=%async_computation.3 | async-start | bytes 65536 | tf_op jit(solution)/shard_map/all_to_all | solution.py:179
Sparse Core Ops, SparseCore 0:
  52.0 61.9 reduce-scatter.3
